TPU v7x, 32 devices: a whole 2x2x4 slice. The times are simulated.
32 devices in a mesh: ia: 4 (over x, core), ja: 2 (over y), ka: 4 (over z).
Axes of the slice: x: 2, y: 2, z: 4, core: 2. Of those that a mesh axis runs over, the one named last changes fastest.
Arguments:
- tensor: float32 [128, 256, 512], P('ia', 'ja', 'ka'), may hold values from -200 to 200
- factor_b: float32 [256, 4, 96], P(('ja', 'ka')), may hold values from -4 to 4
- factor_c: float32 [512, 4, 96], P(('ka', 'ja')), may hold values from -4 to 4
Outputs:
- factor_a: float32 [128, 4, 96], P(('ia', 'ja', 'ka'))
- weights: float32 [4, 96], replicated
All inputs are finite; a program needn't handle non-finite values.
Results may differ from a plain program's by a relative error of at most 0.0003.
Values sent between devices are 32-bit elements; how exact they have to be, the bound alone decides.
A program may use at most 64 MiB of HBM per device.

v0:
```python
import jax
import jax.numpy as jnp
from jax import lax
from jax.sharding import PartitionSpec as P

highest = lax.Precision.HIGHEST


def gram_of(rows):
    return jnp.einsum(
        "jsr,jsq->srq", rows, rows, precision=highest, preferred_element_type=jnp.float32
    )


def solve_normal(rows, gram_b, gram_c):
    columns = []
    for member in range(rows.shape[1]):
        normal_mat = gram_b[member] * gram_c[member]
        factor_l = jnp.linalg.cholesky(normal_mat)
        right_side = rows[:, member, :].T
        lower_sol = lax.linalg.triangular_solve(factor_l, right_side, left_side=True, lower=True)
        upper_sol = lax.linalg.triangular_solve(
            factor_l, lower_sol, left_side=True, lower=True, transpose_a=True
        )
        columns.append(upper_sol.T)
    return jnp.stack(columns, axis=1)


def shards(tensor, factor_b, factor_c):
    rows_i, rows_j, rows_k = tensor.shape
    starts, col_count = (factor_b.shape[1], factor_b.shape[2])
    width = starts * col_count
    c_block = lax.all_gather(factor_c, "ja", axis=0, tiled=True)
    partial_value = jnp.dot(
        tensor.reshape(rows_i * rows_j, rows_k),
        c_block.reshape(rows_k, width),
        precision=highest,
        preferred_element_type=jnp.float32,
    ).reshape(rows_i, rows_j, width)
    piece = lax.all_gather(factor_b, "ka", axis=0, tiled=True)
    gram_sum = jnp.zeros((starts, col_count, col_count), jnp.float32)
    count = piece.shape[0]
    flat_rows = piece.reshape(count, width)
    mttkrp = jnp.einsum(
        "ijr,jr->ir",
        partial_value,
        flat_rows,
        precision=highest,
        preferred_element_type=jnp.float32,
    )
    mttkrp, gram_rows = (mttkrp, gram_sum)
    gram_b, gram_c = lax.psum((gram_of(factor_b), gram_of(factor_c)), ("ja", "ka"))
    owned = lax.psum_scatter(mttkrp, ("ja", "ka"), scatter_dimension=0, tiled=True)
    owned = owned.reshape(owned.shape[0], starts, col_count)
    factor_raw = solve_normal(owned, gram_b, gram_c)
    squares = jnp.sum(factor_raw * factor_raw, axis=0)
    total = lax.psum(squares, ("ia", "ja", "ka"))
    row_total = rows_i * lax.axis_size("ia")
    weights = jnp.sqrt(total / row_total + 1e-06)
    return (factor_raw / weights[None], weights)


def solution(mesh):
    in_specs = (P("ia", "ja", "ka"), P(("ja", "ka"), None, None), P(("ka", "ja"), None, None))
    out_specs = (P(("ia", "ja", "ka"), None, None), P())
    return jax.shard_map(shards, mesh=mesh, in_specs=in_specs, out_specs=out_specs, check_vma=False)
```

profile of v0, /device:TPU:0, one launch (start us, length us, event | category | flops | bytes accessed | tf_op | source)
XLA Modules:
  0.0 222.9 jit_solution(2822683292989447386)
XLA Ops:
  7.2 2.3 %fusion = f32[4,96,96]{1,2,0:T(8,128)} fusion(f32[64,4,96]{2,1,0:T(4,128)} %param.10), kind=kOutput, calls=%fused_computation.4 | convolution fusion | flops 28311552 | bytes 245760 | tf_op jit(solution)/shard_map/jsr,jsq->srq/dot_general | solution.py:10
  9.5 2.1 fusion.2
  11.6 7.4 %all_gather.6 = f32[128,4,96]{2,1,0:T(4,128)S(1)} all-gather(f32[64,4,96]{2,1,0:T(4,128)} %param.10), channel_id=1, replica_groups=mesh['ia'=4,'ja'=2,'ka'=4] {'ja'}, dimensions={0}, use_global_device_ids=true | all-gather | bytes 294912 | tf_op jit(solution)/shard_map/all_gather | solution.py:33
  19.1 15.1 %all_gather.7 = f32[128,4,96]{2,1,0:T(4,128)S(1)} all-gather(f32[32,4,96]{2,1,0:T(4,128)} %param.9), channel_id=1, replica_groups=mesh['ia'=4,'ja'=2,'ka'=4] {'ka'}, dimensions={0}, use_global_device_ids=true | all-gather | bytes 245760 | tf_op jit(solution)/shard_map/all_gather | solution.py:40
  34.3 7.1 %fusion.28 = f32[32,128,384]{2,1,0:T(8,128)} fusion(f32[32,128,128]{2,1,0:T(8,128)S(1)} %copy-done, f32[128,384,1]{0,1,2:T(8,128)S(1)} %bitcast.130), kind=kOutput, calls=%fused_computation.63 | convolution fusion | flops 2415919104 | bytes 8585216 | tf_op jit(solution)/shard_map/dot_general | solution.py:34
  41.3 6.7 %copy.46 = f32[32,128,384]{1,0,2:T(8,128)} copy(f32[32,128,384]{2,1,0:T(8,128)} %fusion.28) | data formatting | bytes 12582912 | tf_op jit(solution)/shard_map/dot_general | solution.py:34
  48.2 11.9 %fusion.29 = f32[384,1,32]{2,1,0:T(1,128)S(1)} fusion(f32[32,128,384]{1,0,2:T(8,128)} %copy.46, f32[128,384,1]{0,2,1:T(1,128)S(1)} %bitcast.124), kind=kOutput, calls=%fused_computation.64 | convolution fusion | flops 18874368 | bytes 6537216 | tf_op jit(solution)/shard_map/ijr,jr->ir/dot_general | solution.py:44
  60.0 0.6 dynamic-slice
  61.3 41.9 %all-reduce = f32[32,384]{0,1:T(8,128)S(1)} all-reduce(f32[32,384]{0,1:T(8,128)S(1)} %bitcast.125), channel_id=2, replica_groups=mesh['ia'=4,'ja'=2,'ka'=4] {'ja','ka'}, use_global_device_ids=true, to_apply=%region_4.0.clone | all-reduce | flops 12288 | bytes 98304
  103.4 1.0 fusion.24
  104.7 1.0 fusion.15
  105.7 8.8 %cholesky.107 = f32[96,96]{1,0:T(8,128)S(1)} custom-call(f32[96,96]{1,0:T(8,128)S(1)} %get-tuple-element.14), custom_call_target="Cholesky" | custom-call | tf_op jit(solution)/shard_map/jit(cholesky)/cholesky | solution.py:19
  114.5 0.6 compare_reduce_fusion
  115.2 0.7 fusion.7
  115.9 7.4 %custom-call.21 = f32[1,96,96]{1,2,0:T(8,128)S(1)} custom-call(f32[1,96,96]{2,1,0:T(8,128)S(1)} %fusion.7), custom_call_target="InvertDiagBlocksLowerTriangular" | custom-call | tf_op jit(solution)/shard_map/triangular_solve/custom-call.2 | solution.py:22
  123.2 0.2 fusion.8
  123.6 8.8 %cholesky.96 = f32[96,96]{1,0:T(8,128)S(1)} custom-call(f32[96,96]{1,0:T(8,128)S(1)} %get-tuple-element.15), custom_call_target="Cholesky" | custom-call | tf_op jit(solution)/shard_map/jit(cholesky)/cholesky | solution.py:19
  132.5 0.6 compare_reduce_fusion.1
  133.1 0.7 fusion.6
  133.8 7.4 %custom-call.19 = f32[1,96,96]{1,2,0:T(8,128)S(1)} custom-call(f32[1,96,96]{2,1,0:T(8,128)S(1)} %fusion.6), custom_call_target="InvertDiagBlocksLowerTriangular" | custom-call | tf_op jit(solution)/shard_map/triangular_solve/custom-call.2 | solution.py:22
  141.1 0.2 fusion.9
  141.5 8.8 %cholesky.85 = f32[96,96]{1,0:T(8,128)S(1)} custom-call(f32[96,96]{1,0:T(8,128)S(1)} %get-tuple-element.16), custom_call_target="Cholesky" | custom-call | tf_op jit(solution)/shard_map/jit(cholesky)/cholesky | solution.py:19
  150.4 0.6 compare_reduce_fusion.2
  151.0 0.7 fusion.5
  151.7 7.4 %custom-call.17 = f32[1,96,96]{1,2,0:T(8,128)S(1)} custom-call(f32[1,96,96]{2,1,0:T(8,128)S(1)} %fusion.5), custom_call_target="InvertDiagBlocksLowerTriangular" | custom-call | tf_op jit(solution)/shard_map/triangular_solve/custom-call.2 | solution.py:22
  159.5 9.0 %cholesky.74 = f32[96,96]{1,0:T(8,128)S(1)} custom-call(f32[96,96]{1,0:T(8,128)S(1)} %get-tuple-element.13), custom_call_target="Cholesky" | custom-call | tf_op jit(solution)/shard_map/jit(cholesky)/cholesky | solution.py:19
  168.5 0.6 compare_reduce_fusion.3
  169.2 0.7 fusion.4
  169.8 7.4 %custom-call.15 = f32[1,96,96]{1,2,0:T(8,128)S(1)} custom-call(f32[1,96,96]{2,1,0:T(8,128)S(1)} %fusion.4), custom_call_target="InvertDiagBlocksLowerTriangular" | custom-call | tf_op jit(solution)/shard_map/triangular_solve/custom-call.2 | solution.py:22
  177.2 0.2 fusion.11
  177.6 37.8 %psum.23 = f32[4,96]{1,0:T(4,128)S(1)} all-reduce(f32[4,96]{1,0:T(4,128)S(1)} %multiply_reduce_fusion), channel_id=1, replica_groups=mesh['ia'=4,'ja'=2,'ka'=4] {'ia','ja','ka'}, use_global_device_ids=true, to_apply=%region_6.10 | all-reduce | flops 384 | bytes 3072 | tf_op jit(solution)/shard_map/psum | solution.py:57
  215.5 0.6 copy.42
  (28 shorter events, 2.0 us)
Async XLA Ops:
  7.2 27.1 %copy-start = (f32[32,128,128]{2,1,0:T(8,128)S(1)}, f32[32,128,128]{2,1,0:T(8,128)}, u32[]{:S(2)}) copy-start(f32[32,128,128]{2,1,0:T(8,128)} %param.8) | copy-start | bytes 6291460
  7.2 96.2 %all-reduce.4.cloned.1.call-start = ((), (), s32[]{:S(2)}) async-start(), calls=%async_computation | async-start | bytes 786432 | tf_op jit(solution)/shard_map/psum | solution.py:52
  48.0 12.0 %copy-start.2 = (u32[32]{0:T(128)S(1)}, u32[32]{0:T(128)}, u32[]{:S(2)}) copy-start(u32[32]{0:T(128)} %constant.41) | copy-start | bytes 388
  215.4 0.6 copy-start.1
Sparse Core Ops, SparseCore 0:
  11.8 75.5 all-reduce.3
where the time goes:
time: 223 us
  blocking collectives  102 us (46%)
  other arithmetic  72.3 us (32%)
  matrix products  24.9 us (11%)
  between operations  14.9 us (7%)
  local copies, waits for them, and re-layouts  8.59 us (4%)
    unnamed x1, blocking collectives  41.9 us
    another operation x12, other arithmetic, solve_normal(): factor_l = jnp.linalg.cholesky(normal_mat)  38.1 us
    psum x1, blocking collectives, shards(): total = lax.psum(squares, ('ia', 'ja', 'ka'))  37.8 us
    another operation x8, other arithmetic, solve_normal(): lax.linalg.triangular_solve(factor_l, lower_sol, left_side=True, lower=Tr...  32 us
    all_gather x1, blocking collectives, shards(): piece = lax.all_gather(factor_b, 'ka', axis=0, tiled=True)  15.1 us
    dot_general x1, matrix products, shards(): jnp.einsum('ijr,jr->ir', partial_value, flat_rows, precision=highest, pre...  11.9 us
    all_gather x1, blocking collectives, shards(): c_block = lax.all_gather(factor_c, 'ja', axis=0, tiled=True)  7.42 us
    dot_general x1, matrix products, shards(): jnp.dot(tensor.reshape(rows_i * rows_j, rows_k), c_block.reshape(rows_k,...  7.07 us
  transfers between devices with their start and end apart: 1, of which 0 were waited for; matrix products, arithmetic and copies ran while one was open for 12% of the time, Pallas kernels for 0%

commit v1 on v0

--- a/solution.py
+++ b/solution.py
@@ -54,7 +54,7 @@
     owned = owned.reshape(owned.shape[0], starts, col_count)
     factor_raw = solve_normal(owned, gram_b, gram_c)
     squares = jnp.sum(factor_raw * factor_raw, axis=0)
-    total = lax.psum(squares, ("ia", "ja", "ka"))
+    total = jnp.sum(lax.all_gather(squares, ("ia", "ja", "ka")), axis=0)
     row_total = rows_i * lax.axis_size("ia")
     weights = jnp.sqrt(total / row_total + 1e-06)
     return (factor_raw / weights[None], weights)

time: 223 us -> 249 us (1.12)
  blocking collectives: 102 us -> 128 us
    all_gather x0 -> x1, blocking collectives: none -> 63.8 us  [shards(): total = jnp.sum(lax.all_gather(squares, ('ia', 'ja', 'ka')), axis=0)]
    psum x1 -> x0, blocking collectives: 37.8 us -> none  [shards(): total = lax.psum(squares, ('ia', 'ja', 'ka'))]
  transfers between devices with their start and end apart: 1 -> 1, of which waited for: 0 -> 0; matrix products, arithmetic and copies ran while one was open for 12% -> 11% of each run, Pallas kernels for 0% -> 0%
where the time goes in v1:
time: 249 us
  blocking collectives  128 us (51%)
  other arithmetic  72.3 us (29%)
  matrix products  24.9 us (10%)
  between operations  14.9 us (6%)
  local copies, waits for them, and re-layouts  8.59 us (3%)
    all_gather x1, blocking collectives, shards(): total = jnp.sum(lax.all_gather(squares, ('ia', 'ja', 'ka')), axis=0)  63.8 us
    unnamed x1, blocking collectives  41.9 us
    another operation x12, other arithmetic, solve_normal(): factor_l = jnp.linalg.cholesky(normal_mat)  38.1 us
    another operation x8, other arithmetic, solve_normal(): lax.linalg.triangular_solve(factor_l, lower_sol, left_side=True, lower=Tr...  32 us
    all_gather x1, blocking collectives, shards(): piece = lax.all_gather(factor_b, 'ka', axis=0, tiled=True)  15.1 us
    dot_general x1, matrix products, shards(): jnp.einsum('ijr,jr->ir', partial_value, flat_rows, precision=highest, pre...  11.9 us
    all_gather x1, blocking collectives, shards(): c_block = lax.all_gather(factor_c, 'ja', axis=0, tiled=True)  7.42 us
    dot_general x1, matrix products, shards(): jnp.dot(tensor.reshape(rows_i * rows_j, rows_k), c_block.reshape(rows_k,...  7.07 us
  transfers between devices with their start and end apart: 1, of which 0 were waited for; matrix products, arithmetic and copies ran while one was open for 11% of the time, Pallas kernels for 0%

profile of v1, /device:TPU:0, one launch (start us, length us, event | category | flops | bytes accessed | tf_op | source)
XLA Modules:
  0.0 249.0 jit_solution(1509567454850531868)
XLA Ops:
  7.2 2.3 fusion
  9.5 2.1 fusion.2
  11.6 7.4 %all_gather.12 = f32[128,4,96]{2,1,0:T(4,128)S(1)} all-gather(f32[64,4,96]{2,1,0:T(4,128)} %param.10), channel_id=1, replica_groups=mesh['ia'=4,'ja'=2,'ka'=4] {'ja'}, dimensions={0}, use_global_device_ids=true | all-gather | bytes 294912 | tf_op jit(solution)/shard_map/all_gather | solution.py:33
  19.1 15.1 %all_gather.13 = f32[128,4,96]{2,1,0:T(4,128)S(1)} all-gather(f32[32,4,96]{2,1,0:T(4,128)} %param.9), channel_id=1, replica_groups=mesh['ia'=4,'ja'=2,'ka'=4] {'ka'}, dimensions={0}, use_global_device_ids=true | all-gather | bytes 245760 | tf_op jit(solution)/shard_map/all_gather | solution.py:40
  34.3 7.1 %fusion.28 = f32[32,128,384]{2,1,0:T(8,128)} fusion(f32[32,128,128]{2,1,0:T(8,128)S(1)} %copy-done, f32[128,384,1]{0,1,2:T(8,128)S(1)} %bitcast.131), kind=kOutput, calls=%fused_computation.63 | convolution fusion | flops 2415919104 | bytes 8585216 | tf_op jit(solution)/shard_map/dot_general | solution.py:34
  41.3 6.7 %copy.46 = f32[32,128,384]{1,0,2:T(8,128)} copy(f32[32,128,384]{2,1,0:T(8,128)} %fusion.28) | data formatting | bytes 12582912 | tf_op jit(solution)/shard_map/dot_general | solution.py:34
  48.2 11.9 %fusion.29 = f32[384,1,32]{2,1,0:T(1,128)S(1)} fusion(f32[32,128,384]{1,0,2:T(8,128)} %copy.46, f32[128,384,1]{0,2,1:T(1,128)S(1)} %bitcast.125), kind=kOutput, calls=%fused_computation.64 | convolution fusion | flops 18874368 | bytes 6537216 | tf_op jit(solution)/shard_map/ijr,jr->ir/dot_general | solution.py:44
  60.0 0.6 dynamic-slice
  61.3 41.9 %all-reduce = f32[32,384]{0,1:T(8,128)S(1)} all-reduce(f32[32,384]{0,1:T(8,128)S(1)} %bitcast.126), channel_id=3, replica_groups=mesh['ia'=4,'ja'=2,'ka'=4] {'ja','ka'}, use_global_device_ids=true, to_apply=%region_4.0.clone | all-reduce | flops 12288 | bytes 98304
  103.4 1.0 fusion.24
  104.7 1.0 fusion.15
  105.7 8.8 %cholesky.107 = f32[96,96]{1,0:T(8,128)S(1)} custom-call(f32[96,96]{1,0:T(8,128)S(1)} %get-tuple-element.14), custom_call_target="Cholesky" | custom-call | tf_op jit(solution)/shard_map/jit(cholesky)/cholesky | solution.py:19
  114.5 0.6 compare_reduce_fusion
  115.2 0.7 fusion.7
  115.9 7.4 %custom-call.21 = f32[1,96,96]{1,2,0:T(8,128)S(1)} custom-call(f32[1,96,96]{2,1,0:T(8,128)S(1)} %fusion.7), custom_call_target="InvertDiagBlocksLowerTriangular" | custom-call | tf_op jit(solution)/shard_map/triangular_solve/custom-call.2 | solution.py:22
  123.2 0.2 fusion.8
  123.6 8.8 %cholesky.96 = f32[96,96]{1,0:T(8,128)S(1)} custom-call(f32[96,96]{1,0:T(8,128)S(1)} %get-tuple-element.15), custom_call_target="Cholesky" | custom-call | tf_op jit(solution)/shard_map/jit(cholesky)/cholesky | solution.py:19
  132.5 0.6 compare_reduce_fusion.1
  133.1 0.7 fusion.6
  133.8 7.4 %custom-call.19 = f32[1,96,96]{1,2,0:T(8,128)S(1)} custom-call(f32[1,96,96]{2,1,0:T(8,128)S(1)} %fusion.6), custom_call_target="InvertDiagBlocksLowerTriangular" | custom-call | tf_op jit(solution)/shard_map/triangular_solve/custom-call.2 | solution.py:22
  141.1 0.2 fusion.9
  141.5 8.8 %cholesky.85 = f32[96,96]{1,0:T(8,128)S(1)} custom-call(f32[96,96]{1,0:T(8,128)S(1)} %get-tuple-element.16), custom_call_target="Cholesky" | custom-call | tf_op jit(solution)/shard_map/jit(cholesky)/cholesky | solution.py:19
  150.4 0.6 compare_reduce_fusion.2
  151.0 0.7 fusion.5
  151.7 7.4 %custom-call.17 = f32[1,96,96]{1,2,0:T(8,128)S(1)} custom-call(f32[1,96,96]{2,1,0:T(8,128)S(1)} %fusion.5), custom_call_target="InvertDiagBlocksLowerTriangular" | custom-call | tf_op jit(solution)/shard_map/triangular_solve/custom-call.2 | solution.py:22
  159.5 9.0 %cholesky.74 = f32[96,96]{1,0:T(8,128)S(1)} custom-call(f32[96,96]{1,0:T(8,128)S(1)} %get-tuple-element.13), custom_call_target="Cholesky" | custom-call | tf_op jit(solution)/shard_map/jit(cholesky)/cholesky | solution.py:19
  168.5 0.6 compare_reduce_fusion.3
  169.2 0.7 fusion.4
  169.8 7.4 %custom-call.15 = f32[1,96,96]{1,2,0:T(8,128)S(1)} custom-call(f32[1,96,96]{2,1,0:T(8,128)S(1)} %fusion.4), custom_call_target="InvertDiagBlocksLowerTriangular" | custom-call | tf_op jit(solution)/shard_map/triangular_solve/custom-call.2 | solution.py:22
  177.2 0.2 fusion.11
  177.6 63.8 %all-gather.1 = f32[32,4,96]{2,1,0:T(4,128)S(1)} all-gather(f32[1,4,96]{2,1,0:T(4,128)S(1)} %bitcast.132), channel_id=2, replica_groups=mesh['ia'=4,'ja'=2,'ka'=4] {'ia','ja','ka'}, dimensions={0}, use_global_device_ids=true | all-gather | bytes 50688 | tf_op jit(solution)/shard_map/all_gather | solution.py:57
  241.5 0.6 copy.42
  (29 shorter events, 2.0 us)
Async XLA Ops:
  7.2 27.1 %copy-start = (f32[32,128,128]{2,1,0:T(8,128)S(1)}, f32[32,128,128]{2,1,0:T(8,128)}, u32[]{:S(2)}) copy-start(f32[32,128,128]{2,1,0:T(8,128)} %param.8) | copy-start | bytes 6291460
  7.2 96.2 %all-reduce.4.cloned.1.call-start = ((), (), s32[]{:S(2)}) async-start(), calls=%async_computation | async-start | bytes 786432 | tf_op jit(solution)/shard_map/psum | solution.py:52
  48.0 12.0 %copy-start.2 = (u32[32]{0:T(128)S(1)}, u32[32]{0:T(128)}, u32[]{:S(2)}) copy-start(u32[32]{0:T(128)} %constant.41) | copy-start | bytes 388
  241.5 0.6 copy-start.1
Sparse Core Ops, SparseCore 0:
  11.8 75.5 all-reduce.3
